TPU v7x, 32 devices: a whole 2x2x4 slice. The times are simulated.
32 devices in a mesh: seq: 4 (over y, x), tp: 8 (over z, core).
Axes of the slice: x: 2, y: 2, z: 4, core: 2. Of those that a mesh axis runs over, the one named last changes fastest.
Arguments:
- tokens: bfloat16 [4096, 4096], P('seq'), may hold values from -32 to 32
- w_query: bfloat16 [4096, 2048], P(None, 'tp'), may hold values from -0.109375 to 0.109375
- w_key: bfloat16 [4096, 512], P(None, 'tp'), may hold values from -0.078125 to 0.078125
- w_value: bfloat16 [4096, 512], P(None, 'tp'), may hold values from -0.09375 to 0.09375
- w_out: bfloat16 [2048, 4096], P('tp'), may hold values from -0.1875 to 0.1875
- seg_ids: int32 [4096], replicated, may hold values from 0 to 31, as said below
- owner_counts: int32 [8], replicated, may hold values from 1 to 8, 32 in all
- centroids: bfloat16 [16384, 4096], P('seq', 'tp'), may hold values from -1.5 to 1.5
- pool_gain: float32 [4096], P('tp'), may hold values from 0.1 to 1.9
- assign: int32 [32], replicated, may hold values from 0 to 16383
Outputs:
- distances: float32 [64, 16384], P('tp', 'seq')
- updated: float32 [16384, 4096], P('seq', 'tp')
Inputs may be any that keep to these rules, and one draw needn't show every extreme that they name: `seg_ids`: ids never fall along the sequence; every id occurs; one instruction spans exactly 4065 tokens. `owner_counts`: the counts sum to 32; one owner holds exactly 8 rows.
All inputs are finite; a program needn't handle non-finite values.
Results may differ from a plain program's by a relative error of at most 0.0007.
Values may be sent and summed in bfloat16 or wider, within the bound.
No kernel may reach another device: no remote copies, remote signals or barrier semaphores. Data moves between devices by JAX's collectives and lax.ppermute only.
A program may use at most 192 MiB of HBM per device.

v0:
```python
import math
import jax
import jax.numpy as jnp
from jax import lax
from jax.sharding import PartitionSpec as P

HD = 128
WINDOW = 4096
QBLOCK = 512
rope_theta = 10000.0
norm_eps = 1e-06


def from_partner(x, axis, apart):
    return lax.ppermute(x, axis, [(i, i ^ 1 << apart) for i in range(lax.axis_size(axis))])


def from_behind(value, axis, steps):
    count = lax.axis_size(axis)
    leading, last = (max(0, -steps), min(count, count - steps))
    return lax.ppermute(value, axis, [(source, source + steps) for source in range(leading, last)])


def rotate_pairs(vectors, positions, first_pair, head_size):
    cols = vectors.shape[-1]
    pair_index = (first_pair + jnp.arange(cols // 2)).astype(jnp.float32)
    inverse = jnp.exp(-(2.0 * pair_index / head_size) * math.log(rope_theta))
    angles = positions.astype(jnp.float32)[:, None] * inverse[None, :]
    cosine = jnp.cos(angles)[:, None, :]
    sine = jnp.sin(angles)[:, None, :]
    paired = vectors.reshape(vectors.shape[:-1] + (cols // 2, 2))
    even_part = paired[..., 0]
    odd_part = paired[..., 1]
    turned = jnp.stack(
        [even_part * cosine - odd_part * sine, even_part * sine + odd_part * cosine], -1
    )
    return turned.reshape(vectors.shape)


def shards(
    tokens, w_query, w_key, w_value, w_out, seg_ids, owner_counts, centroids, pool_gain, assign
):
    tok_rows, model_width = tokens.shape
    half_cols = w_key.shape[1]
    heads_here = w_query.shape[1] // HD
    rank_seq = lax.axis_index("seq")
    rank_tp = lax.axis_index("tp")
    tp_total = lax.axis_size("tp")
    positions = rank_seq * tok_rows + jnp.arange(tok_rows, dtype=jnp.int32)
    queries = rotate_pairs(
        jnp.dot(tokens, w_query, preferred_element_type=jnp.float32).reshape(
            tok_rows, heads_here, HD
        ),
        positions,
        0,
        HD,
    ).astype(jnp.bfloat16)
    lower_first = rank_tp % 2 == 0
    key_half = jnp.dot(tokens, w_key, preferred_element_type=jnp.float32).reshape(
        tok_rows, 1, half_cols
    )
    key_half = rotate_pairs(key_half, positions, rank_tp % 2 * (half_cols // 2), HD).reshape(
        tok_rows, half_cols
    )
    value_half = jnp.dot(tokens, w_value, preferred_element_type=jnp.float32)
    own_pair = jnp.concatenate([key_half.astype(jnp.bfloat16), value_half.astype(jnp.bfloat16)], -1)
    partner = from_partner(own_pair, "tp", 0)
    front = jnp.where(lower_first, own_pair, partner)
    back = jnp.where(lower_first, partner, own_pair)
    key_rows = jnp.concatenate([front[:, :half_cols], back[:, :half_cols]], -1)
    value_rows = jnp.concatenate([front[:, half_cols:], back[:, half_cols:]], -1)
    kv_local = jnp.concatenate([key_rows, value_rows], -1)
    halo_shards = WINDOW // tok_rows
    reach = min(halo_shards, lax.axis_size("seq") - 1)
    pieces = [kv_local]
    for back_step in range(1, reach + 1):
        pieces.insert(0, from_behind(kv_local, "seq", back_step))
    if halo_shards > reach:
        pieces.insert(0, jnp.zeros(((halo_shards - reach) * tok_rows, 2 * HD), jnp.bfloat16))
    kv_window = jnp.concatenate(pieces, 0)
    pad_ids = jnp.concatenate([jnp.full((WINDOW,), -1, jnp.int32), seg_ids], 0)
    distance_grid = jnp.arange(QBLOCK)[:, None] + WINDOW - jnp.arange(WINDOW + QBLOCK)[None, :]
    outputs = []
    for block_index in range(tok_rows // QBLOCK):
        q_start = block_index * QBLOCK
        q_block = queries[q_start : q_start + QBLOCK]
        kv_block = kv_window[q_start : q_start + WINDOW + QBLOCK]
        q_ids = lax.dynamic_slice_in_dim(seg_ids, rank_seq * tok_rows + q_start, QBLOCK, 0)
        k_ids = lax.dynamic_slice_in_dim(pad_ids, rank_seq * tok_rows + q_start, WINDOW + QBLOCK, 0)
        allowed = (
            (distance_grid >= 0) & (distance_grid < WINDOW) & (q_ids[:, None] == k_ids[None, :])
        )
        scores = jnp.einsum(
            "qhd,kd->hqk", q_block, kv_block[:, :HD], preferred_element_type=jnp.float32
        ) * HD ** (-0.5)
        scores = jnp.where(allowed[None], scores, -1e30)
        highest = jnp.max(scores, axis=-1, keepdims=True)
        weights = jnp.exp(scores - highest)
        soft_weights = (weights / jnp.sum(weights, axis=-1, keepdims=True)).astype(jnp.bfloat16)
        head_out = jnp.einsum(
            "hqk,kd->qhd", soft_weights, kv_block[:, HD:], preferred_element_type=jnp.float32
        ).astype(jnp.bfloat16)
        outputs.append(head_out.reshape(QBLOCK, heads_here * HD))
    attention = jnp.concatenate(outputs, 0)
    seg_total = assign.shape[0]
    member = (
        lax.dynamic_slice_in_dim(seg_ids, rank_seq * tok_rows, tok_rows, 0)[:, None]
        == jnp.arange(seg_total, dtype=jnp.int32)[None, :]
    )
    member_float = member.astype(jnp.float32)
    member_half = member.astype(jnp.bfloat16)
    feat_cols = model_width // tp_total
    token_cols = lax.dynamic_slice_in_dim(tokens, rank_tp * feat_cols, feat_cols, 1)
    pooled_tokens = lax.dot_general(
        member_half, token_cols, (((0,), (0,)), ((), ())), preferred_element_type=jnp.float32
    )
    mixed_cols = lax.psum_scatter(
        lax.dot_general(
            w_out, attention, (((0,), (1,)), ((), ())), preferred_element_type=jnp.float32
        ),
        "tp",
        scatter_dimension=0,
        tiled=True,
    )
    pooled_mixed = lax.dot_general(
        member_float, mixed_cols, (((0,), (1,)), ((), ())), precision=lax.Precision.HIGHEST
    )
    seg_sums = lax.psum(pooled_tokens + pooled_mixed, "seq")
    counts = jnp.sum(
        (seg_ids[:, None] == jnp.arange(seg_total, dtype=jnp.int32)[None, :]).astype(jnp.float32),
        axis=0,
    )
    pooled = seg_sums / counts[:, None]
    square_sums = lax.psum(jnp.sum(pooled * pooled, axis=1), "tp")
    mean_square = square_sums / model_width
    embedding = pooled * lax.rsqrt(mean_square + norm_eps)[:, None] * pool_gain[None, :]
    cross_term = lax.dot_general(
        embedding.astype(jnp.bfloat16),
        centroids,
        (((1,), (1,)), ((), ())),
        preferred_element_type=jnp.float32,
    )
    cent_float = centroids.astype(jnp.float32)
    cent_norm = jnp.sum(cent_float * cent_float, axis=1)
    row_terms = (cent_norm[None, :] - 2.0 * cross_term) / model_width**0.5
    owners = owner_counts.shape[0]
    capacity = 2 * seg_total // owners
    starts = jnp.cumsum(owner_counts) - owner_counts
    slot_index = jnp.arange(capacity, dtype=jnp.int32)
    slot_rows = (starts[:, None] + slot_index[None, :]).reshape(-1)
    slot_valid = (slot_index[None, :] < owner_counts[:, None]).reshape(-1)
    selector = (
        (slot_rows[:, None] == jnp.arange(seg_total, dtype=jnp.int32)[None, :])
        & slot_valid[:, None]
    ).astype(jnp.float32)
    slot_terms = jnp.dot(selector, row_terms, precision=lax.Precision.HIGHEST)
    distances = lax.psum_scatter(slot_terms, "tp", scatter_dimension=0, tiled=True)
    cent_rows = centroids.shape[0]
    cent_ids = rank_seq * cent_rows + jnp.arange(cent_rows, dtype=jnp.int32)
    chosen = (assign[None, :] == cent_ids[:, None]).astype(jnp.float32)
    cent_sums = jnp.dot(chosen, embedding, precision=lax.Precision.HIGHEST)
    cent_counts = jnp.sum(chosen, axis=1)
    updated = (cent_float + cent_sums) / (1.0 + cent_counts)[:, None]
    return (distances, updated)


def solution(mesh):
    in_specs = (
        P("seq", None),
        P(None, "tp"),
        P(None, "tp"),
        P(None, "tp"),
        P("tp", None),
        P(),
        P(),
        P("seq", "tp"),
        P("tp"),
        P(),
    )
    out_specs = (P("tp", "seq"), P("seq", "tp"))
    return jax.shard_map(shards, mesh=mesh, in_specs=in_specs, out_specs=out_specs, check_vma=False)
```

profile of v0, /device:TPU:0, one launch (start us, length us, event | category | flops | bytes accessed | tf_op | source)
XLA Modules:
  0.0 416.3 jit_solution(12850956107057330214)
XLA Ops:
  7.3 6.3 %fusion.69 = f32[1024,64]{0,1:T(8,128)S(1)} fusion(bf16[1024,4096]{1,0:T(8,128)(2,1)} %param.10, bf16[4096,64]{0,1:T(8,128)(2,1)} %param.12), kind=kOutput, calls=%fused_computation.125 | convolution fusion | flops 536870912 | bytes 9175040 | tf_op jit(solution)/shard_map/dot_general | solution.py:59
  14.8 6.0 %convolution_convert_fusion = bf16[1024,64]{0,1:T(8,128)(2,1)S(1)} fusion(bf16[1024,4096]{1,0:T(8,128)(2,1)} %param.10, bf16[4096,64]{0,1:T(8,128)(2,1)S(1)} %copy-done.4), kind=kOutput, calls=%fused_computation.40 | convolution fusion | flops 536936448 | bytes 9043968 | tf_op jit(solution)/shard_map/dot_general | solution.py:65
  23.8 7.3 %fusion.70 = f32[1024,256]{0,1:T(8,128)} fusion(bf16[1024,4096]{1,0:T(8,128)(2,1)} %param.10, bf16[4096,256]{1,0:T(8,128)(2,1)} %param.11), kind=kOutput, calls=%fused_computation.126 | convolution fusion | flops 2147483648 | bytes 11534336 | tf_op jit(solution)/shard_map/dot_general | solution.py:51
  33.2 7.0 %compare_and_fusion.1 = (pred[512,4608]{0,1:T(8,128)(4,1)}, pred[512,4608]{0,1:T(8,128)(4,1)}) fusion(s32[512]{0:T(512)S(1)} %get-tuple-element.20, s32[512]{0:T(512)S(1)} %get-tuple-element.32, s32[4608]{0:T(1024)S(1)} %get-tuple-element.18, s32[4608]{0:T(1024)S(1)} %get-tuple-element.19, s32[512]{0:T(512)S(1)} %get-tuple-element.21), kind=kLoop, calls=%fused_computation.23 | loop fusion | flops 18874368 | bytes 4761600 | tf_op jit(solution)/shard_map/and | solution.py:91
  42.2 5.4 %collective-permute-start.1 = (bf16[1024,256]{0,1:T(8,128)(2,1)S(1)}, bf16[1024,256]{0,1:T(8,128)(2,1)S(1)}, u32[]{:S(2)}, u32[]{:S(2)}) collective-permute-start(bf16[1024,256]{0,1:T(8,128)(2,1)S(1)} %pad_maximum_fusion), channel_id=1, source_target_pairs={{0,24},{1,25},{2,26},{3,27},{4,28},{5,29},{6,30},{7,31}} | collective-permute-start | bytes 1572872 | tf_op jit(solution)/shard_map/ppermute | solution.py:21
  48.9 2.7 collective-permute-start.3
  53.2 6.6 %collective-permute-done.1 = bf16[1024,256]{0,1:T(8,128)(2,1)S(1)} collective-permute-done((bf16[1024,256]{0,1:T(8,128)(2,1)S(1)}, bf16[1024,256]{0,1:T(8,128)(2,1)S(1)}, u32[]{:S(2)}, u32[]{:S(2)}) %collective-permute-start.1) | collective-permute-done | bytes 524320 | tf_op jit(solution)/shard_map/ppermute | solution.py:21
  59.8 12.1 %collective-permute-done.2 = bf16[1024,256]{0,1:T(8,128)(2,1)S(1)} collective-permute-done((bf16[1024,256]{0,1:T(8,128)(2,1)S(1)}, bf16[1024,256]{0,1:T(8,128)(2,1)S(1)}, u32[]{:S(2)}, u32[]{:S(2)}) %collective-permute-start.2) | collective-permute-done | bytes 524320 | tf_op jit(solution)/shard_map/ppermute | solution.py:21
  72.1 8.3 %fusion.22 = f32[4608,512,2]{1,0,2:T(8,128)} fusion(bf16[5120,256]{0,1:T(8,128)(2,1)S(1)} %constant_dynamic-update-slice_fusion, bf16[512,2,128]{0,1,2:T(2,128)(2,1)S(1)} %bitcast.64), kind=kOutput, calls=%fused_computation.38 | convolution fusion | flops 1207959552 | bytes 20316160 | tf_op jit(solution)/shard_map/qhd,kd->hqk/dot_general | solution.py:93
  80.4 2.6 fusion.21
  83.0 21.7 %fusion.68 = (f32[2,512]{1,0:T(2,128)S(1)}, f32[2,512,4608]{1,2,0:T(8,128)}) fusion(f32[4608,512,2]{1,0,2:T(8,128)} %fusion.22, pred[512,4608]{0,1:T(8,128)(4,1)} %get-tuple-element.24), kind=kOutput, calls=%fused_computation.124 | output fusion | flops 28316160 | bytes 40112128 | tf_op jit(solution)/shard_map/sub | solution.py:98
  104.8 8.9 %fusion.20 = bf16[128,2,512]{2,0,1:T(8,128)(2,1)} fusion(f32[2,512,4608]{1,2,0:T(8,128)} %get-tuple-element.29, f32[2,512]{1,0:T(2,128)S(1)} %get-tuple-element.28, bf16[5120,256]{0,1:T(8,128)(2,1)} %copy-done.1), kind=kOutput, calls=%fused_computation.33 | convolution fusion | flops 1217527808 | bytes 20320256 | tf_op jit(solution)/shard_map/hqk,kd->qhd/dot_general | solution.py:100
  113.6 13.4 %fusion.67 = (f32[2,512]{1,0:T(2,128)S(1)}, f32[2,512,4608]{1,2,0:T(8,128)}) fusion(f32[4608,512,2]{1,0,2:T(8,128)S(1)} %fusion.21, pred[512,4608]{0,1:T(8,128)(4,1)} %get-tuple-element.25), kind=kOutput, calls=%fused_computation.123 | output fusion | flops 28316160 | bytes 40112128 | tf_op jit(solution)/shard_map/sub | solution.py:98
  127.0 8.2 %fusion.19 = bf16[128,2,512]{2,0,1:T(8,128)(2,1)S(1)} fusion(f32[2,512,4608]{1,2,0:T(8,128)} %get-tuple-element.27, f32[2,512]{1,0:T(2,128)S(1)} %get-tuple-element.26, bf16[5120,256]{0,1:T(8,128)(2,1)} %copy-done.1), kind=kOutput, calls=%fused_computation.32 | convolution fusion | flops 1217527808 | bytes 20320256 | tf_op jit(solution)/shard_map/hqk,kd->qhd/dot_general | solution.py:100
  135.2 8.1 %convolution_bitcast_fusion = f32[4096,1024]{0,1:T(8,128)} fusion(bf16[256,4096]{1,0:T(8,128)(2,1)S(1)} %copy-done, bf16[512,256]{0,1:T(8,128)(2,1)S(1)} %bitcast.66, bf16[512,256]{0,1:T(8,128)(2,1)S(1)} %bitcast.65), kind=kOutput, calls=%fused_computation.26 | convolution fusion | flops 2148532224 | bytes 19398656 | tf_op jit(solution)/shard_map/dot_general | solution.py:118
  144.5 3.1 fusion.15
  147.6 165.5 %reduce-scatter.3.cloned.1.call-done = f32[512,1024]{0,1:T(8,128)} async-done(((f32[4096,1024]{0,1:T(8,128)}), f32[512,1024]{0,1:T(8,128)}) %reduce-scatter.3.cloned.1.call-update) | async-done | bytes 2097168 | tf_op jit(solution)/shard_map/reduce_scatter | solution.py:117
  313.1 2.6 fusion.29
  315.6 2.3 convolution_add_fusion
  318.2 39.8 %all-reduce.3.cloned.1.call-done = f32[32,512]{1,0:T(8,128)} async-done(((f32[32,512]{1,0:T(8,128)}), f32[32,512]{1,0:T(8,128)}) %all-reduce.3.cloned.1.call-update) | async-done | bytes 65552 | tf_op jit(solution)/shard_map/psum | solution.py:128
  359.0 16.0 %psum.15 = f32[32]{0:T(128)S(1)} all-reduce(f32[32]{0:T(128)S(1)} %multiply_reduce_fusion), channel_id=1, replica_groups=mesh['seq'=4,'tp'=8] {'tp'}, use_global_device_ids=true, to_apply=%region_10.11 | all-reduce | flops 32 | bytes 256 | tf_op jit(solution)/shard_map/psum | solution.py:134
  375.0 3.6 fusion.18
  380.4 8.0 %fusion.16 = f32[4096,512]{1,0:T(8,128)} fusion(bf16[4096,512]{1,0:T(8,128)(2,1)} %param.17, f32[4096]{0:T(1024)S(1)} %broadcast_add_fusion, s32[4096]{0:T(1024)S(1)} %iota_add_fusion, s32[32]{0:T(128)S(1)} %copy-done.8, f32[512]{0:T(512)S(1)} %copy-done.7, f32[32]{0:T(128)S(1)} %add_rsqrt_fusion, f32[32,512]{1,0:T(8,128)} %all-reduce.3.cloned.1.call-done, ...), kind=kOutput, calls=%fused_computation.28 | convolution fusion | flops 811778048 | bytes 12683648 | tf_op jit(solution)/shard_map/dot_general | solution.py:161
  388.4 21.4 %reduce-scatter.5.cloned.1.call-done = f32[8,4096]{1,0:T(8,128)} async-done(((f32[64,4096]{1,0:T(8,128)}), f32[8,4096]{1,0:T(8,128)}) %reduce-scatter.5.cloned.1.call-update) | async-done | bytes 131088 | tf_op jit(solution)/shard_map/reduce_scatter | solution.py:157
  (69 shorter events, 15.4 us)
Async XLA Ops:
  7.2 128.0 %copy-start = (bf16[256,4096]{1,0:T(8,128)(2,1)S(1)}, bf16[256,4096]{1,0:T(8,128)(2,1)}, u32[]{:S(2)}) copy-start(bf16[256,4096]{1,0:T(8,128)(2,1)} %param.14) | copy-start | bytes 6291460
  7.2 7.6 %copy-start.4 = (bf16[4096,64]{0,1:T(8,128)(2,1)S(1)}, bf16[4096,64]{0,1:T(8,128)(2,1)}, u32[]{:S(2)}) copy-start(bf16[4096,64]{0,1:T(8,128)(2,1)} %param.13) | copy-start | bytes 1572868
  7.2 305.9 %reduce-scatter.3.cloned.1.call-start = ((), (), s32[]{:S(2)}) async-start(), calls=%async_computation.2 | async-start | bytes 18874368 | tf_op jit(solution)/shard_map/reduce_scatter | solution.py:117
  21.5 19.5 %collective-permute-start = (bf16[1024,128]{0,1:T(8,128)(2,1)}, bf16[1024,128]{0,1:T(8,128)(2,1)}, u32[]{:S(2)}, u32[]{:S(2)}) collective-permute-start(bf16[1024,128]{0,1:T(8,128)(2,1)} %pad_maximum_fusion.2), channel_id=1, source_target_pairs={{0,1},{1,0},{2,3},{3,2},{4,5},{5,4},{6,7},{7,6},{8,9},{9,8},{10,11... | collective-permute-start | bytes 786440 | tf_op jit(solution)/shard_map/ppermute | solution.py:15
  23.8 9.2 %copy-start.6 = (s32[4096]{0:T(1024)S(1)}, s32[4096]{0:T(1024)}, u32[]{:S(2)}) copy-start(s32[4096]{0:T(1024)} %param.15) | copy-start | bytes 49156
  33.0 18.6 %copy-start.2 = (f32[1024,64]{0,1:T(8,128)S(1)}, f32[1024,64]{0,1:T(8,128)}, u32[]{:S(2)}) copy-start(f32[1024,64]{0,1:T(8,128)} %get-tuple-element.22) | copy-start | bytes 786436
  33.0 18.6 %copy-start.3 = (f32[1024,64]{0,1:T(8,128)S(1)}, f32[1024,64]{0,1:T(8,128)}, u32[]{:S(2)}) copy-start(f32[1024,64]{0,1:T(8,128)} %get-tuple-element.23) | copy-start | bytes 786436
  42.2 17.6 %collective-permute-start.1 = (bf16[1024,256]{0,1:T(8,128)(2,1)S(1)}, bf16[1024,256]{0,1:T(8,128)(2,1)S(1)}, u32[]{:S(2)}, u32[]{:S(2)}) collective-permute-start(bf16[1024,256]{0,1:T(8,128)(2,1)S(1)} %pad_maximum_fusion), channel_id=1, source_target_pairs={{0,24},{1,25},{2,26},{3,27},{4,28},{5,29},{6,30},{7,31}} | collective-permute-start | bytes 1572872 | tf_op jit(solution)/shard_map/ppermute | solution.py:21
  47.6 24.4 %collective-permute-start.2 = (bf16[1024,256]{0,1:T(8,128)(2,1)S(1)}, bf16[1024,256]{0,1:T(8,128)(2,1)S(1)}, u32[]{:S(2)}, u32[]{:S(2)}) collective-permute-start(bf16[1024,256]{0,1:T(8,128)(2,1)S(1)} %pad_maximum_fusion), channel_id=1, source_target_pairs={{0,16},{8,24},{1,17},{9,25},{2,18},{10,26},{3,19},{11,27},{4,20},{... | collective-permute-start | bytes 1572872 | tf_op jit(solution)/shard_map/ppermute | solution.py:21
  48.9 23.1 %collective-permute-start.3 = (bf16[1024,256]{0,1:T(8,128)(2,1)S(1)}, bf16[1024,256]{0,1:T(8,128)(2,1)S(1)}, u32[]{:S(2)}, u32[]{:S(2)}) collective-permute-start(bf16[1024,256]{0,1:T(8,128)(2,1)S(1)} %pad_maximum_fusion), channel_id=1, source_target_pairs={{0,8},{8,16},{16,24},{1,9},{9,17},{17,25},{2,10},{10,18},{18,26},{... | collective-permute-start | bytes 1572872 | tf_op jit(solution)/shard_map/ppermute | solution.py:21
  72.1 8.3 %copy-start.1 = (bf16[5120,256]{0,1:T(8,128)(2,1)}, bf16[5120,256]{0,1:T(8,128)(2,1)S(1)}, u32[]{:S(2)}) copy-start(bf16[5120,256]{0,1:T(8,128)(2,1)S(1)} %constant_dynamic-update-slice_fusion) | copy-start | bytes 7864324
  127.0 8.2 %copy-start.5 = (bf16[128,2,512]{2,0,1:T(8,128)(2,1)S(1)}, bf16[128,2,512]{2,0,1:T(8,128)(2,1)}, u32[]{:S(2)}) copy-start(bf16[128,2,512]{2,0,1:T(8,128)(2,1)} %fusion.20) | copy-start | bytes 786436
  143.3 0.7 copy-start.9
  143.3 231.7 %copy-start.7 = (f32[512]{0:T(512)S(1)}, f32[512]{0:T(512)}, u32[]{:S(2)}) copy-start(f32[512]{0:T(512)} %param.18) | copy-start | bytes 6148
  143.4 236.9 %copy-start.8 = (s32[32]{0:T(128)S(1)}, s32[32]{0:T(128)}, u32[]{:S(2)}) copy-start(s32[32]{0:T(128)} %param.19) | copy-start | bytes 388
  143.4 214.6 %all-reduce.3.cloned.1.call-start = ((), (), s32[]{:S(2)}) async-start(), calls=%async_computation.3 | async-start | bytes 131072 | tf_op jit(solution)/shard_map/psum | solution.py:128
  318.0 91.7 %reduce-scatter.5.cloned.1.call-start = ((), (), s32[]{:S(2)}) async-start(), calls=%async_computation.4 | async-start | bytes 1179648 | tf_op jit(solution)/shard_map/reduce_scatter | solution.py:157
Sparse Core Ops, SparseCore 0:
  143.5 169.5 reduce-scatter.2
  318.1 39.8 all-reduce.2
  380.3 29.3 reduce-scatter.4
where the time goes:
time: 417 us; the launch traced here: 416 us
  waiting for transfers between devices  245 us (59%)
  matrix products  73.8 us (18%)
  other arithmetic  52.9 us (13%)
  blocking collectives  16 us (4%)
  between operations  14.1 us (3%)
  starting transfers between devices  9.94 us (2%)
  local copies, waits for them, and re-layouts  4.25 us (1%)
    reduce_scatter x1, waiting for transfers between devices, shards(): lax.psum_scatter(lax.dot_general(w_out, attention, (((0,), (1,)), ((), ()...  165 us
    psum x1, waiting for transfers between devices, shards(): seg_sums = lax.psum(pooled_tokens + pooled_mixed, 'seq')  39.8 us
    sub x2, other arithmetic, shards(): weights = jnp.exp(scores - highest)  35.1 us
    reduce_scatter x1, waiting for transfers between devices, shards(): lax.psum_scatter(slot_terms, 'tp', scatter_dimension=0, tiled=True)  21.4 us
    ppermute x3, waiting for transfers between devices, from_behind(): lax.ppermute(value, axis, [(source, source + steps) for source in range(l...  18.7 us
    dot_general x2, matrix products, shards(): jnp.einsum('hqk,kd->qhd', soft_weights, kv_block[:, HD:], preferred_eleme...  17 us
    psum x1, blocking collectives, shards(): square_sums = lax.psum(jnp.sum(pooled * pooled, axis=1), 'tp')  16 us
    dot_general x2, matrix products, shards(): jnp.einsum('qhd,kd->hqk', q_block, kv_block[:, :HD], preferred_element_ty...  11 us
  transfers between devices with their start and end apart: 7, of which 5 were waited for; matrix products, arithmetic and copies ran while one was open for 8% of the time, Pallas kernels for 0%

commit v1 on v0

--- a/solution.py
+++ b/solution.py
@@ -125,7 +125,7 @@
     pooled_mixed = lax.dot_general(
         member_float, mixed_cols, (((0,), (1,)), ((), ())), precision=lax.Precision.HIGHEST
     )
-    seg_sums = lax.psum(pooled_tokens + pooled_mixed, "seq")
+    seg_sums = jnp.sum(lax.all_gather(pooled_tokens + pooled_mixed, "seq"), axis=0)
     counts = jnp.sum(
         (seg_ids[:, None] == jnp.arange(seg_total, dtype=jnp.int32)[None, :]).astype(jnp.float32),
         axis=0,

time: 417 us -> 382 us (0.916)
  waiting for transfers between devices: 245 us -> 205 us
  blocking collectives: 16 us -> 22.6 us
    psum x1 -> x0, waiting for transfers between devices: 39.8 us -> none  [shards(): seg_sums = lax.psum(pooled_tokens + pooled_mixed, 'seq')]
    all_gather x0 -> x1, blocking collectives: none -> 8.96 us  [shards(): lax.all_gather(pooled_tokens + pooled_mixed, 'seq')]
  transfers between devices with their start and end apart: 7 -> 6, of which waited for: 5 -> 4; matrix products, arithmetic and copies ran while one was open for 8% -> 9% of each run, Pallas kernels for 0% -> 0%
where the time goes in v1:
time: 382 us
  waiting for transfers between devices  205 us (54%)
  matrix products  73.1 us (19%)
  other arithmetic  52.1 us (14%)
  blocking collectives  22.6 us (6%)
  between operations  14.4 us (4%)
  starting transfers between devices  9.9 us (3%)
  local copies, waits for them, and re-layouts  4.25 us (1%)
    reduce_scatter x1, waiting for transfers between devices, shards(): lax.psum_scatter(lax.dot_general(w_out, attention, (((0,), (1,)), ((), ()...  165 us
    sub x2, other arithmetic, shards(): weights = jnp.exp(scores - highest)  35.1 us
    reduce_scatter x1, waiting for transfers between devices, shards(): lax.psum_scatter(slot_terms, 'tp', scatter_dimension=0, tiled=True)  21.5 us
    ppermute x3, waiting for transfers between devices, from_behind(): lax.ppermute(value, axis, [(source, source + steps) for source in range(l...  18.7 us
    dot_general x2, matrix products, shards(): jnp.einsum('hqk,kd->qhd', soft_weights, kv_block[:, HD:], preferred_eleme...  17 us
    psum x1, blocking collectives, shards(): square_sums = lax.psum(jnp.sum(pooled * pooled, axis=1), 'tp')  13.6 us
    dot_general x2, matrix products, shards(): jnp.einsum('qhd,kd->hqk', q_block, kv_block[:, :HD], preferred_element_ty...  11 us
    ppermute x3, starting transfers between devices, from_behind(): lax.ppermute(value, axis, [(source, source + steps) for source in range(l...  9.37 us
  transfers between devices with their start and end apart: 6, of which 4 were waited for; matrix products, arithmetic and copies ran while one was open for 9% of the time, Pallas kernels for 0%

profile of v1, /device:TPU:0, one launch (start us, length us, event | category | flops | bytes accessed | tf_op | source)
XLA Modules:
  0.0 381.8 jit_solution(13312479673074202998)
XLA Ops:
  7.3 6.3 %fusion.69 = f32[1024,64]{0,1:T(8,128)S(1)} fusion(bf16[1024,4096]{1,0:T(8,128)(2,1)} %param.10, bf16[4096,64]{0,1:T(8,128)(2,1)} %param.12), kind=kOutput, calls=%fused_computation.125 | convolution fusion | flops 536870912 | bytes 9175040 | tf_op jit(solution)/shard_map/dot_general | solution.py:59
  14.8 6.0 %convolution_convert_fusion = bf16[1024,64]{0,1:T(8,128)(2,1)S(1)} fusion(bf16[1024,4096]{1,0:T(8,128)(2,1)} %param.10, bf16[4096,64]{0,1:T(8,128)(2,1)S(1)} %copy-done.4), kind=kOutput, calls=%fused_computation.40 | convolution fusion | flops 536936448 | bytes 9043968 | tf_op jit(solution)/shard_map/dot_general | solution.py:65
  23.8 7.3 %fusion.70 = f32[1024,256]{0,1:T(8,128)} fusion(bf16[1024,4096]{1,0:T(8,128)(2,1)} %param.10, bf16[4096,256]{1,0:T(8,128)(2,1)} %param.11), kind=kOutput, calls=%fused_computation.126 | convolution fusion | flops 2147483648 | bytes 11534336 | tf_op jit(solution)/shard_map/dot_general | solution.py:51
  31.1 1.8 reshape_reshape.8
  33.2 7.0 %compare_and_fusion.1 = (pred[512,4608]{0,1:T(8,128)(4,1)}, pred[512,4608]{0,1:T(8,128)(4,1)}) fusion(s32[512]{0:T(512)S(1)} %get-tuple-element.20, s32[512]{0:T(512)S(1)} %get-tuple-element.32, s32[4608]{0:T(1024)S(1)} %get-tuple-element.18, s32[4608]{0:T(1024)S(1)} %get-tuple-element.19, s32[512]{0:T(512)S(1)} %get-tuple-element.21), kind=kLoop, calls=%fused_computation.23 | loop fusion | flops 18874368 | bytes 4761600 | tf_op jit(solution)/shard_map/and | solution.py:91
  42.2 5.4 %collective-permute-start.1 = (bf16[1024,256]{0,1:T(8,128)(2,1)S(1)}, bf16[1024,256]{0,1:T(8,128)(2,1)S(1)}, u32[]{:S(2)}, u32[]{:S(2)}) collective-permute-start(bf16[1024,256]{0,1:T(8,128)(2,1)S(1)} %pad_maximum_fusion), channel_id=1, source_target_pairs={{0,24},{1,25},{2,26},{3,27},{4,28},{5,29},{6,30},{7,31}} | collective-permute-start | bytes 1572872 | tf_op jit(solution)/shard_map/ppermute | solution.py:21
  48.9 2.7 collective-permute-start.3
  53.2 6.6 %collective-permute-done.1 = bf16[1024,256]{0,1:T(8,128)(2,1)S(1)} collective-permute-done((bf16[1024,256]{0,1:T(8,128)(2,1)S(1)}, bf16[1024,256]{0,1:T(8,128)(2,1)S(1)}, u32[]{:S(2)}, u32[]{:S(2)}) %collective-permute-start.1) | collective-permute-done | bytes 524320 | tf_op jit(solution)/shard_map/ppermute | solution.py:21
  59.8 12.1 %collective-permute-done.2 = bf16[1024,256]{0,1:T(8,128)(2,1)S(1)} collective-permute-done((bf16[1024,256]{0,1:T(8,128)(2,1)S(1)}, bf16[1024,256]{0,1:T(8,128)(2,1)S(1)}, u32[]{:S(2)}, u32[]{:S(2)}) %collective-permute-start.2) | collective-permute-done | bytes 524320 | tf_op jit(solution)/shard_map/ppermute | solution.py:21
  72.1 8.3 %fusion.22 = f32[4608,512,2]{1,0,2:T(8,128)} fusion(bf16[5120,256]{0,1:T(8,128)(2,1)S(1)} %constant_dynamic-update-slice_fusion, bf16[512,2,128]{0,1,2:T(2,128)(2,1)S(1)} %bitcast.65), kind=kOutput, calls=%fused_computation.38 | convolution fusion | flops 1207959552 | bytes 20316160 | tf_op jit(solution)/shard_map/qhd,kd->hqk/dot_general | solution.py:93
  80.4 2.6 fusion.21
  83.0 21.7 %fusion.68 = (f32[2,512]{1,0:T(2,128)S(1)}, f32[2,512,4608]{1,2,0:T(8,128)}) fusion(f32[4608,512,2]{1,0,2:T(8,128)} %fusion.22, pred[512,4608]{0,1:T(8,128)(4,1)} %get-tuple-element.24), kind=kOutput, calls=%fused_computation.124 | output fusion | flops 28316160 | bytes 40112128 | tf_op jit(solution)/shard_map/sub | solution.py:98
  104.8 8.9 %fusion.20 = bf16[128,2,512]{2,0,1:T(8,128)(2,1)} fusion(f32[2,512,4608]{1,2,0:T(8,128)} %get-tuple-element.29, f32[2,512]{1,0:T(2,128)S(1)} %get-tuple-element.28, bf16[5120,256]{0,1:T(8,128)(2,1)} %copy-done.1), kind=kOutput, calls=%fused_computation.33 | convolution fusion | flops 1217527808 | bytes 20320256 | tf_op jit(solution)/shard_map/hqk,kd->qhd/dot_general | solution.py:100
  113.6 13.4 %fusion.67 = (f32[2,512]{1,0:T(2,128)S(1)}, f32[2,512,4608]{1,2,0:T(8,128)}) fusion(f32[4608,512,2]{1,0,2:T(8,128)S(1)} %fusion.21, pred[512,4608]{0,1:T(8,128)(4,1)} %get-tuple-element.25), kind=kOutput, calls=%fused_computation.123 | output fusion | flops 28316160 | bytes 40112128 | tf_op jit(solution)/shard_map/sub | solution.py:98
  127.0 8.2 %fusion.19 = bf16[128,2,512]{2,0,1:T(8,128)(2,1)S(1)} fusion(f32[2,512,4608]{1,2,0:T(8,128)} %get-tuple-element.27, f32[2,512]{1,0:T(2,128)S(1)} %get-tuple-element.26, bf16[5120,256]{0,1:T(8,128)(2,1)} %copy-done.1), kind=kOutput, calls=%fused_computation.32 | convolution fusion | flops 1217527808 | bytes 20320256 | tf_op jit(solution)/shard_map/hqk,kd->qhd/dot_general | solution.py:100
  135.2 8.1 %convolution_bitcast_fusion = f32[4096,1024]{0,1:T(8,128)} fusion(bf16[256,4096]{1,0:T(8,128)(2,1)S(1)} %copy-done, bf16[512,256]{0,1:T(8,128)(2,1)S(1)} %bitcast.68, bf16[512,256]{0,1:T(8,128)(2,1)S(1)} %bitcast.67), kind=kOutput, calls=%fused_computation.26 | convolution fusion | flops 2148532224 | bytes 19398656 | tf_op jit(solution)/shard_map/dot_general | solution.py:118
  144.7 3.1 fusion.15
  147.8 165.3 %reduce-scatter.3.cloned.1.call-done = f32[512,1024]{0,1:T(8,128)} async-done(((f32[4096,1024]{0,1:T(8,128)}), f32[512,1024]{0,1:T(8,128)}) %reduce-scatter.3.cloned.1.call-update) | async-done | bytes 2097168 | tf_op jit(solution)/shard_map/reduce_scatter | solution.py:117
  313.1 2.6 fusion.29
  317.3 9.0 %all-gather = f32[128,512]{1,0:T(8,128)S(1)} all-gather(f32[32,512]{1,0:T(8,128)S(1)} %convolution_add_fusion), channel_id=2, replica_groups=mesh['seq'=4,'tp'=8] {'seq'}, dimensions={0}, use_global_device_ids=true | all-gather | bytes 327680 | tf_op jit(solution)/shard_map/all_gather | solution.py:128
  326.5 13.6 %psum.7 = f32[32]{0:T(128)S(1)} all-reduce(f32[32]{0:T(128)S(1)} %multiply_reduce_fusion), channel_id=1, replica_groups=mesh['seq'=4,'tp'=8] {'tp'}, use_global_device_ids=true, to_apply=%region_10.11 | all-reduce | flops 32 | bytes 256 | tf_op jit(solution)/shard_map/psum | solution.py:134
  340.1 3.5 fusion.18
  345.5 8.0 %fusion.16 = f32[4096,512]{1,0:T(8,128)} fusion(bf16[4096,512]{1,0:T(8,128)(2,1)} %param.17, f32[4096]{0:T(1024)S(1)} %broadcast_add_fusion, s32[4096]{0:T(1024)S(1)} %iota_add_fusion, s32[32]{0:T(128)S(1)} %copy-done.8, f32[512]{0:T(512)S(1)} %copy-done.7, f32[32]{0:T(128)S(1)} %add_rsqrt_fusion, f32[32,512]{1,0:T(8,128)S(1)} %reduce_sum.66, ...), kind=kOutput, calls=%fused_computation.28 | convolution fusion | flops 811778048 | bytes 12683648 | tf_op jit(solution)/shard_map/dot_general | solution.py:161
  353.4 21.5 %reduce-scatter.5.cloned.1.call-done = f32[8,4096]{1,0:T(8,128)} async-done(((f32[64,4096]{1,0:T(8,128)}), f32[8,4096]{1,0:T(8,128)}) %reduce-scatter.5.cloned.1.call-update) | async-done | bytes 131088 | tf_op jit(solution)/shard_map/reduce_scatter | solution.py:157
  (68 shorter events, 14.4 us)
Async XLA Ops:
  7.2 128.0 %copy-start = (bf16[256,4096]{1,0:T(8,128)(2,1)S(1)}, bf16[256,4096]{1,0:T(8,128)(2,1)}, u32[]{:S(2)}) copy-start(bf16[256,4096]{1,0:T(8,128)(2,1)} %param.14) | copy-start | bytes 6291460
  7.2 7.6 %copy-start.4 = (bf16[4096,64]{0,1:T(8,128)(2,1)S(1)}, bf16[4096,64]{0,1:T(8,128)(2,1)}, u32[]{:S(2)}) copy-start(bf16[4096,64]{0,1:T(8,128)(2,1)} %param.13) | copy-start | bytes 1572868
  7.2 305.9 %reduce-scatter.3.cloned.1.call-start = ((), (), s32[]{:S(2)}) async-start(), calls=%async_computation.2 | async-start | bytes 18874368 | tf_op jit(solution)/shard_map/reduce_scatter | solution.py:117
  21.5 19.5 %collective-permute-start = (bf16[1024,128]{0,1:T(8,128)(2,1)}, bf16[1024,128]{0,1:T(8,128)(2,1)}, u32[]{:S(2)}, u32[]{:S(2)}) collective-permute-start(bf16[1024,128]{0,1:T(8,128)(2,1)} %pad_maximum_fusion.2), channel_id=1, source_target_pairs={{0,1},{1,0},{2,3},{3,2},{4,5},{5,4},{6,7},{7,6},{8,9},{9,8},{10,11... | collective-permute-start | bytes 786440 | tf_op jit(solution)/shard_map/ppermute | solution.py:15
  23.8 9.2 %copy-start.6 = (s32[4096]{0:T(1024)S(1)}, s32[4096]{0:T(1024)}, u32[]{:S(2)}) copy-start(s32[4096]{0:T(1024)} %param.15) | copy-start | bytes 49156
  33.0 18.6 %copy-start.2 = (f32[1024,64]{0,1:T(8,128)S(1)}, f32[1024,64]{0,1:T(8,128)}, u32[]{:S(2)}) copy-start(f32[1024,64]{0,1:T(8,128)} %get-tuple-element.22) | copy-start | bytes 786436
  33.0 18.6 %copy-start.3 = (f32[1024,64]{0,1:T(8,128)S(1)}, f32[1024,64]{0,1:T(8,128)}, u32[]{:S(2)}) copy-start(f32[1024,64]{0,1:T(8,128)} %get-tuple-element.23) | copy-start | bytes 786436
  42.2 17.6 %collective-permute-start.1 = (bf16[1024,256]{0,1:T(8,128)(2,1)S(1)}, bf16[1024,256]{0,1:T(8,128)(2,1)S(1)}, u32[]{:S(2)}, u32[]{:S(2)}) collective-permute-start(bf16[1024,256]{0,1:T(8,128)(2,1)S(1)} %pad_maximum_fusion), channel_id=1, source_target_pairs={{0,24},{1,25},{2,26},{3,27},{4,28},{5,29},{6,30},{7,31}} | collective-permute-start | bytes 1572872 | tf_op jit(solution)/shard_map/ppermute | solution.py:21
  47.6 24.4 %collective-permute-start.2 = (bf16[1024,256]{0,1:T(8,128)(2,1)S(1)}, bf16[1024,256]{0,1:T(8,128)(2,1)S(1)}, u32[]{:S(2)}, u32[]{:S(2)}) collective-permute-start(bf16[1024,256]{0,1:T(8,128)(2,1)S(1)} %pad_maximum_fusion), channel_id=1, source_target_pairs={{0,16},{8,24},{1,17},{9,25},{2,18},{10,26},{3,19},{11,27},{4,20},{... | collective-permute-start | bytes 1572872 | tf_op jit(solution)/shard_map/ppermute | solution.py:21
  48.9 23.1 %collective-permute-start.3 = (bf16[1024,256]{0,1:T(8,128)(2,1)S(1)}, bf16[1024,256]{0,1:T(8,128)(2,1)S(1)}, u32[]{:S(2)}, u32[]{:S(2)}) collective-permute-start(bf16[1024,256]{0,1:T(8,128)(2,1)S(1)} %pad_maximum_fusion), channel_id=1, source_target_pairs={{0,8},{8,16},{16,24},{1,9},{9,17},{17,25},{2,10},{10,18},{18,26},{... | collective-permute-start | bytes 1572872 | tf_op jit(solution)/shard_map/ppermute | solution.py:21
  72.1 8.3 %copy-start.1 = (bf16[5120,256]{0,1:T(8,128)(2,1)}, bf16[5120,256]{0,1:T(8,128)(2,1)S(1)}, u32[]{:S(2)}) copy-start(bf16[5120,256]{0,1:T(8,128)(2,1)S(1)} %constant_dynamic-update-slice_fusion) | copy-start | bytes 7864324
  127.0 8.2 %copy-start.5 = (bf16[128,2,512]{2,0,1:T(8,128)(2,1)S(1)}, bf16[128,2,512]{2,0,1:T(8,128)(2,1)}, u32[]{:S(2)}) copy-start(bf16[128,2,512]{2,0,1:T(8,128)(2,1)} %fusion.20) | copy-start | bytes 786436
  143.3 0.7 copy-start.9
  143.3 196.8 %copy-start.7 = (f32[512]{0:T(512)S(1)}, f32[512]{0:T(512)}, u32[]{:S(2)}) copy-start(f32[512]{0:T(512)} %param.18) | copy-start | bytes 6148
  143.4 202.0 %copy-start.8 = (s32[32]{0:T(128)S(1)}, s32[32]{0:T(128)}, u32[]{:S(2)}) copy-start(s32[32]{0:T(128)} %param.19) | copy-start | bytes 388
  143.4 231.6 %reduce-scatter.5.cloned.1.call-start = ((), (), s32[]{:S(2)}) async-start(), calls=%async_computation.3 | async-start | bytes 1179648 | tf_op jit(solution)/shard_map/reduce_scatter | solution.py:157
Sparse Core Ops, SparseCore 0:
  143.5 169.5 reduce-scatter.2
  345.4 29.4 reduce-scatter.4
